TPU v7x, 512 devices: a whole 4x4x16 slice. The times are simulated.
512 devices in a mesh: blk: 32 (over z_lo, x, core), group: 16 (over y, z_hi).
Axes of the slice: x: 4, y: 4, z: 16 (z_hi: 4, z_lo: 4; z = z_hi * 4 + z_lo), core: 2. Of those that a mesh axis runs over, the one named last changes fastest.
Arguments:
- queries: bfloat16 [16, 8192, 4096], P('group', 'blk'), may hold values from -30 to 30
- passages: bfloat16 [16, 512, 4096], P('group', 'blk'), may hold values from -7 to 7
- positives: int32 [16, 8192], P('group', 'blk'), may hold values from 0 to 511
- hard_rows: bfloat16 [16, 512, 4096], P('group', 'blk'), may hold values from -6 to 6
- hard_dest: int32 [16, 512, 1], P('group', 'blk'), may hold values from 0 to 15; in each aligned block of 16 rows (0 to 15, 16 to 31, ..., all dimensions but the last counted through in order) at most 2 rows name the same one
Outputs:
- loss_rows: float32 [16, 8192], P('group', 'blk')
- d_queries: bfloat16 [16, 8192, 4096], P('group', 'blk')
- d_passages: bfloat16 [16, 512, 4096], P('group', 'blk')
- d_hard: bfloat16 [16, 512, 4096], P('group', 'blk')
Inputs may be any that keep to these rules, and one draw needn't show every extreme that they name: `hard_dest`: among the 16 hard rows of one device, at most 2 name the same group, and some device reaches 2.
All inputs are finite; a program needn't handle non-finite values.
Results may differ from a plain program's by a relative error of at most 0.0048.
Values may be sent and summed in bfloat16 or wider, within the bound.
No kernel may reach another device: no remote copies, remote signals or barrier semaphores. Data moves between devices by JAX's collectives and lax.ppermute only.
A program may use at most 64 MiB of HBM per device.

v0:
```python
import jax
import jax.numpy as jnp
from jax import lax
from jax.sharding import PartitionSpec as P


def from_behind(x, axis, by):
    count = lax.axis_size(axis)
    return lax.ppermute(x, axis, [(i, (i + by) % count) for i in range(count)])


def body(queries, passages, positives, hard_rows, hard_dest):
    query_rows = queries[0]
    own_passages = passages[0]
    targets = positives[0]
    owned_hard = hard_rows[0]
    routes = hard_dest[0, :, 0]
    groups = lax.axis_size("group")
    blocks = lax.axis_size("blk")
    blk_index = lax.axis_index("blk")
    feat_width = query_rows.shape[1]
    passage_count = own_passages.shape[0]
    hard_count = owned_hard.shape[0]
    total_rows = passage_count * blocks
    score_multiplier = feat_width ** (-0.5)
    largest_score = lax.Precision.HIGHEST
    slot_count = max(2, 2 * hard_count // groups)
    onehot_dest = (routes[:, None] == jnp.arange(groups, dtype=jnp.int32)[None, :]).astype(
        jnp.int32
    )
    ranking = jnp.sum((jnp.cumsum(onehot_dest, axis=0) - onehot_dest) * onehot_dest, axis=1)
    slot_of = routes * slot_count + ranking
    placing = (
        slot_of[None, :] == jnp.arange(groups * slot_count, dtype=jnp.int32)[:, None]
    ).astype(jnp.bfloat16)
    packed = jnp.dot(placing, owned_hard, preferred_element_type=jnp.float32).astype(jnp.bfloat16)
    packed = packed.reshape(groups, slot_count, feat_width)
    live_flags = jnp.sum(placing, axis=1).reshape(groups, slot_count)
    arrived, arrived_flags = (
        lax.all_to_all(packed, "group", split_axis=0, concat_axis=0, tiled=True),
        lax.all_to_all(live_flags, "group", split_axis=0, concat_axis=0, tiled=True),
    )
    received = arrived.reshape(groups * slot_count, feat_width)
    is_live = arrived_flags.reshape(groups * slot_count) > 0.5
    raw_hard = score_multiplier * jnp.einsum(
        "qd,hd->qh", query_rows, received, preferred_element_type=jnp.float32
    )
    negative_scores = jnp.where(is_live[None, :], raw_hard, -jnp.inf)
    hard_top = jnp.max(negative_scores, axis=1)
    received_wide = received.astype(jnp.float32)
    target_hot = (targets[:, None] == jnp.arange(total_rows, dtype=jnp.int32)[None, :]).astype(
        jnp.float32
    )
    gathered = lax.all_gather(own_passages, "blk", axis=0, tiled=True)
    in_scores = score_multiplier * jnp.einsum(
        "qd,pd->qp", query_rows, gathered, preferred_element_type=jnp.float32
    )
    run_top = jnp.maximum(jnp.max(in_scores, axis=1), hard_top)
    run_total = jnp.sum(jnp.exp(in_scores - run_top[:, None]), axis=1) + jnp.sum(
        jnp.exp(negative_scores - run_top[:, None]), axis=1
    )
    log_total = run_top + jnp.log(run_total)
    prob_in = jnp.exp(in_scores - log_total[:, None])
    hard_probability = jnp.exp(negative_scores - log_total[:, None])
    coef_in = prob_in - target_hot
    d_query = score_multiplier * (
        jnp.dot(coef_in, gathered.astype(jnp.float32), precision=largest_score)
        + jnp.dot(hard_probability, received_wide, precision=largest_score)
    )
    loss_rows = log_total - jnp.sum(in_scores * target_hot, axis=1)
    coef_round = coef_in.astype(jnp.bfloat16)

    def contrib(col_start, row_count):
        coef_cols = lax.dynamic_slice_in_dim(coef_round, col_start, row_count, 1)
        return jnp.einsum("qp,qd->pd", coef_cols, query_rows, preferred_element_type=jnp.float32)

    def owner_col(turn_index):
        return (blk_index - turn_index - 1) % blocks * passage_count

    def advance(turn_index, running):
        running = from_behind(running, "blk", 1)
        return running + contrib(owner_col(turn_index), passage_count)

    summed = lax.fori_loop(1, blocks, advance, contrib(owner_col(0), passage_count))
    d_passage = (score_multiplier * summed).astype(jnp.bfloat16)
    hard_exchange_round = hard_probability.astype(jnp.bfloat16)
    slot_grads = (
        score_multiplier
        * jnp.einsum(
            "qh,qd->hd", hard_exchange_round, query_rows, preferred_element_type=jnp.float32
        )
    ).astype(jnp.bfloat16)
    slot_grads = slot_grads.reshape(groups, slot_count, feat_width)
    returned = lax.all_to_all(slot_grads, "group", split_axis=0, concat_axis=0, tiled=True).reshape(
        groups * slot_count, feat_width
    )
    d_owned = jnp.einsum("sh,sd->hd", placing, returned, preferred_element_type=jnp.float32).astype(
        jnp.bfloat16
    )
    return (loss_rows[None], d_query.astype(jnp.bfloat16)[None], d_passage[None], d_owned[None])


def solution(mesh):
    return jax.shard_map(
        body,
        mesh=mesh,
        in_specs=(
            P("group", "blk", None),
            P("group", "blk", None),
            P("group", "blk"),
            P("group", "blk", None),
            P("group", "blk", None),
        ),
        out_specs=(
            P("group", "blk"),
            P("group", "blk", None),
            P("group", "blk", None),
            P("group", "blk", None),
        ),
        check_vma=False,
    )
```

profile of v0, /device:TPU:8, one launch (start us, length us, event | category | flops | bytes accessed | tf_op | source)
XLA Modules:
  0.0 506.8 jit_solution(9961726672704951241)
XLA Ops:
  11.0 18.2 %all-to-all-start = ((bf16[16,1,2]{2,1,0:T(2,128)(2,1)}), bf16[16,1,2]{2,1,0:T(2,128)(2,1)S(1)}, u32[]{:S(2)}, u32[]{:S(2)}) async-start(bf16[16,1,2]{2,1,0:T(2,128)(2,1)} %all_to_all.16), calls=%async_computation | async-start | bytes 16384 | tf_op jit(solution)/shard_map/all_to_all | solution.py:41
  30.4 12.1 %all-to-all-done = bf16[16,1,2]{2,1,0:T(2,128)(2,1)S(1)} async-done(((bf16[16,1,2]{2,1,0:T(2,128)(2,1)}), bf16[16,1,2]{2,1,0:T(2,128)(2,1)S(1)}, u32[]{:S(2)}, u32[]{:S(2)}) %all-to-all-start) | async-done | bytes 96 | tf_op jit(solution)/shard_map/all_to_all | solution.py:41
  42.5 4.8 all-to-all-start.1
  47.4 22.5 %all-to-all-done.1 = bf16[16,2,4096]{2,1,0:T(2,128)(2,1)S(1)} async-done(((bf16[16,2,4096]{2,1,0:T(2,128)(2,1)}), bf16[16,2,4096]{2,1,0:T(2,128)(2,1)S(1)}, u32[]{:S(2)}, u32[]{:S(2)}) %all-to-all-start.1) | async-done | bytes 262176 | tf_op jit(solution)/shard_map/all_to_all | solution.py:40
  70.9 20.0 %all-gather.3.cloned.1.call-done = bf16[1,512,4096]{2,1,0:T(8,128)(2,1)} async-done(((bf16[1,16,4096]{2,1,0:T(8,128)(2,1)}), bf16[1,512,4096]{2,1,0:T(8,128)(2,1)}) %all-gather.3.cloned.1.call-update) | async-done | bytes 4194320 | tf_op jit(solution)/shard_map/all_gather | solution.py:54
  90.9 3.7 fusion.37
  96.2 3.8 fusion.7
  100.0 3.3 fusion.4
  104.2 15.7 %all-to-all-start.2 = ((bf16[16,2,4096]{2,1,0:T(2,128)(2,1)}), bf16[16,2,4096]{2,1,0:T(2,128)(2,1)S(1)}, u32[]{:S(2)}, u32[]{:S(2)}) async-start(bf16[16,2,4096]{2,1,0:T(2,128)(2,1)} %reshape.101), calls=%async_computation.2 | async-start | bytes 524288 | tf_op jit(solution)/shard_map/all_to_all | solution.py:94
  120.4 378.0 %while.15 = (s32[]{:T(128)}, f32[16,4096]{1,0:T(8,128)S(1)}, s32[]{:T(128)}, bf16[256,512]{1,0:T(8,128)(2,1)S(1)}, bf16[256,4096]{1,0:T(8,128)(2,1)S(1)}, /*inde...) while((s32[]{:T(128)}, f32[16,4096]{1,0:T(8,128)S(1)}, ...), condition=%wide.region_9.10_spmd, body=%wide.region_8.9_spmd.sunk | while | flops 33619984 | bytes 3735892 | solution.py:84
  120.4 1.9 collective-permute-start
  122.3 12.9 %collective-permute-done = f32[16,4096]{1,0:T(8,128)S(1)} collective-permute-done((f32[16,4096]{1,0:T(8,128)S(1)}, f32[16,4096]{1,0:T(8,128)S(1)}, u32[]{:S(2)}, u32[]{:S(2)}) %collective-permute-start) | collective-permute-done | bytes 262176 | tf_op jit(solution)/shard_map/while/body/eval_jaxpr/ppermute | solution.py:9
  137.7 10.0 %collective-permute-done = f32[16,4096]{1,0:T(8,128)S(1)} collective-permute-done((f32[16,4096]{1,0:T(8,128)S(1)}, f32[16,4096]{1,0:T(8,128)S(1)}, u32[]{:S(2)}, u32[]{:S(2)}) %collective-permute-start) | collective-permute-done | bytes 262176 | tf_op jit(solution)/shard_map/while/body/eval_jaxpr/ppermute | solution.py:9
  148.2 1.9 collective-permute-start
  150.1 9.6 %collective-permute-done = f32[16,4096]{1,0:T(8,128)S(1)} collective-permute-done((f32[16,4096]{1,0:T(8,128)S(1)}, f32[16,4096]{1,0:T(8,128)S(1)}, u32[]{:S(2)}, u32[]{:S(2)}) %collective-permute-start) | collective-permute-done | bytes 262176 | tf_op jit(solution)/shard_map/while/body/eval_jaxpr/ppermute | solution.py:9
  162.2 9.6 %collective-permute-done = f32[16,4096]{1,0:T(8,128)S(1)} collective-permute-done((f32[16,4096]{1,0:T(8,128)S(1)}, f32[16,4096]{1,0:T(8,128)S(1)}, u32[]{:S(2)}, u32[]{:S(2)}) %collective-permute-start) | collective-permute-done | bytes 262176 | tf_op jit(solution)/shard_map/while/body/eval_jaxpr/ppermute | solution.py:9
  172.3 1.9 collective-permute-start
  174.3 9.6 %collective-permute-done = f32[16,4096]{1,0:T(8,128)S(1)} collective-permute-done((f32[16,4096]{1,0:T(8,128)S(1)}, f32[16,4096]{1,0:T(8,128)S(1)}, u32[]{:S(2)}, u32[]{:S(2)}) %collective-permute-start) | collective-permute-done | bytes 262176 | tf_op jit(solution)/shard_map/while/body/eval_jaxpr/ppermute | solution.py:9
  184.4 1.9 collective-permute-start
  186.3 9.6 %collective-permute-done = f32[16,4096]{1,0:T(8,128)S(1)} collective-permute-done((f32[16,4096]{1,0:T(8,128)S(1)}, f32[16,4096]{1,0:T(8,128)S(1)}, u32[]{:S(2)}, u32[]{:S(2)}) %collective-permute-start) | collective-permute-done | bytes 262176 | tf_op jit(solution)/shard_map/while/body/eval_jaxpr/ppermute | solution.py:9
  196.5 1.9 collective-permute-start
  198.4 9.6 %collective-permute-done = f32[16,4096]{1,0:T(8,128)S(1)} collective-permute-done((f32[16,4096]{1,0:T(8,128)S(1)}, f32[16,4096]{1,0:T(8,128)S(1)}, u32[]{:S(2)}, u32[]{:S(2)}) %collective-permute-start) | collective-permute-done | bytes 262176 | tf_op jit(solution)/shard_map/while/body/eval_jaxpr/ppermute | solution.py:9
  208.5 1.9 collective-permute-start
  210.5 9.6 %collective-permute-done = f32[16,4096]{1,0:T(8,128)S(1)} collective-permute-done((f32[16,4096]{1,0:T(8,128)S(1)}, f32[16,4096]{1,0:T(8,128)S(1)}, u32[]{:S(2)}, u32[]{:S(2)}) %collective-permute-start) | collective-permute-done | bytes 262176 | tf_op jit(solution)/shard_map/while/body/eval_jaxpr/ppermute | solution.py:9
  220.6 1.9 collective-permute-start
  222.6 9.6 %collective-permute-done = f32[16,4096]{1,0:T(8,128)S(1)} collective-permute-done((f32[16,4096]{1,0:T(8,128)S(1)}, f32[16,4096]{1,0:T(8,128)S(1)}, u32[]{:S(2)}, u32[]{:S(2)}) %collective-permute-start) | collective-permute-done | bytes 262176 | tf_op jit(solution)/shard_map/while/body/eval_jaxpr/ppermute | solution.py:9
  234.6 9.6 %collective-permute-done = f32[16,4096]{1,0:T(8,128)S(1)} collective-permute-done((f32[16,4096]{1,0:T(8,128)S(1)}, f32[16,4096]{1,0:T(8,128)S(1)}, u32[]{:S(2)}, u32[]{:S(2)}) %collective-permute-start) | collective-permute-done | bytes 262176 | tf_op jit(solution)/shard_map/while/body/eval_jaxpr/ppermute | solution.py:9
  246.7 9.6 %collective-permute-done = f32[16,4096]{1,0:T(8,128)S(1)} collective-permute-done((f32[16,4096]{1,0:T(8,128)S(1)}, f32[16,4096]{1,0:T(8,128)S(1)}, u32[]{:S(2)}, u32[]{:S(2)}) %collective-permute-start) | collective-permute-done | bytes 262176 | tf_op jit(solution)/shard_map/while/body/eval_jaxpr/ppermute | solution.py:9
  256.8 1.9 collective-permute-start
  258.8 9.6 %collective-permute-done = f32[16,4096]{1,0:T(8,128)S(1)} collective-permute-done((f32[16,4096]{1,0:T(8,128)S(1)}, f32[16,4096]{1,0:T(8,128)S(1)}, u32[]{:S(2)}, u32[]{:S(2)}) %collective-permute-start) | collective-permute-done | bytes 262176 | tf_op jit(solution)/shard_map/while/body/eval_jaxpr/ppermute | solution.py:9
  268.9 1.9 collective-permute-start
  270.9 9.6 %collective-permute-done = f32[16,4096]{1,0:T(8,128)S(1)} collective-permute-done((f32[16,4096]{1,0:T(8,128)S(1)}, f32[16,4096]{1,0:T(8,128)S(1)}, u32[]{:S(2)}, u32[]{:S(2)}) %collective-permute-start) | collective-permute-done | bytes 262176 | tf_op jit(solution)/shard_map/while/body/eval_jaxpr/ppermute | solution.py:9
  281.0 1.9 collective-permute-start
  282.9 9.6 %collective-permute-done = f32[16,4096]{1,0:T(8,128)S(1)} collective-permute-done((f32[16,4096]{1,0:T(8,128)S(1)}, f32[16,4096]{1,0:T(8,128)S(1)}, u32[]{:S(2)}, u32[]{:S(2)}) %collective-permute-start) | collective-permute-done | bytes 262176 | tf_op jit(solution)/shard_map/while/body/eval_jaxpr/ppermute | solution.py:9
  293.1 1.9 collective-permute-start
  295.0 9.6 %collective-permute-done = f32[16,4096]{1,0:T(8,128)S(1)} collective-permute-done((f32[16,4096]{1,0:T(8,128)S(1)}, f32[16,4096]{1,0:T(8,128)S(1)}, u32[]{:S(2)}, u32[]{:S(2)}) %collective-permute-start) | collective-permute-done | bytes 262176 | tf_op jit(solution)/shard_map/while/body/eval_jaxpr/ppermute | solution.py:9
  305.1 1.9 collective-permute-start
  307.1 9.6 %collective-permute-done = f32[16,4096]{1,0:T(8,128)S(1)} collective-permute-done((f32[16,4096]{1,0:T(8,128)S(1)}, f32[16,4096]{1,0:T(8,128)S(1)}, u32[]{:S(2)}, u32[]{:S(2)}) %collective-permute-start) | collective-permute-done | bytes 262176 | tf_op jit(solution)/shard_map/while/body/eval_jaxpr/ppermute | solution.py:9
  319.2 9.6 %collective-permute-done = f32[16,4096]{1,0:T(8,128)S(1)} collective-permute-done((f32[16,4096]{1,0:T(8,128)S(1)}, f32[16,4096]{1,0:T(8,128)S(1)}, u32[]{:S(2)}, u32[]{:S(2)}) %collective-permute-start) | collective-permute-done | bytes 262176 | tf_op jit(solution)/shard_map/while/body/eval_jaxpr/ppermute | solution.py:9
  329.3 1.9 collective-permute-start
  331.2 9.6 %collective-permute-done = f32[16,4096]{1,0:T(8,128)S(1)} collective-permute-done((f32[16,4096]{1,0:T(8,128)S(1)}, f32[16,4096]{1,0:T(8,128)S(1)}, u32[]{:S(2)}, u32[]{:S(2)}) %collective-permute-start) | collective-permute-done | bytes 262176 | tf_op jit(solution)/shard_map/while/body/eval_jaxpr/ppermute | solution.py:9
  341.4 1.9 collective-permute-start
  343.3 9.6 %collective-permute-done = f32[16,4096]{1,0:T(8,128)S(1)} collective-permute-done((f32[16,4096]{1,0:T(8,128)S(1)}, f32[16,4096]{1,0:T(8,128)S(1)}, u32[]{:S(2)}, u32[]{:S(2)}) %collective-permute-start) | collective-permute-done | bytes 262176 | tf_op jit(solution)/shard_map/while/body/eval_jaxpr/ppermute | solution.py:9
  353.4 1.9 collective-permute-start
  355.4 9.6 %collective-permute-done = f32[16,4096]{1,0:T(8,128)S(1)} collective-permute-done((f32[16,4096]{1,0:T(8,128)S(1)}, f32[16,4096]{1,0:T(8,128)S(1)}, u32[]{:S(2)}, u32[]{:S(2)}) %collective-permute-start) | collective-permute-done | bytes 262176 | tf_op jit(solution)/shard_map/while/body/eval_jaxpr/ppermute | solution.py:9
  365.5 1.9 collective-permute-start
  367.5 9.6 %collective-permute-done = f32[16,4096]{1,0:T(8,128)S(1)} collective-permute-done((f32[16,4096]{1,0:T(8,128)S(1)}, f32[16,4096]{1,0:T(8,128)S(1)}, u32[]{:S(2)}, u32[]{:S(2)}) %collective-permute-start) | collective-permute-done | bytes 262176 | tf_op jit(solution)/shard_map/while/body/eval_jaxpr/ppermute | solution.py:9
  377.6 1.9 collective-permute-start
  379.5 9.6 %collective-permute-done = f32[16,4096]{1,0:T(8,128)S(1)} collective-permute-done((f32[16,4096]{1,0:T(8,128)S(1)}, f32[16,4096]{1,0:T(8,128)S(1)}, u32[]{:S(2)}, u32[]{:S(2)}) %collective-permute-start) | collective-permute-done | bytes 262176 | tf_op jit(solution)/shard_map/while/body/eval_jaxpr/ppermute | solution.py:9
  391.6 9.6 %collective-permute-done = f32[16,4096]{1,0:T(8,128)S(1)} collective-permute-done((f32[16,4096]{1,0:T(8,128)S(1)}, f32[16,4096]{1,0:T(8,128)S(1)}, u32[]{:S(2)}, u32[]{:S(2)}) %collective-permute-start) | collective-permute-done | bytes 262176 | tf_op jit(solution)/shard_map/while/body/eval_jaxpr/ppermute | solution.py:9
  401.7 1.9 collective-permute-start
  403.7 9.6 %collective-permute-done = f32[16,4096]{1,0:T(8,128)S(1)} collective-permute-done((f32[16,4096]{1,0:T(8,128)S(1)}, f32[16,4096]{1,0:T(8,128)S(1)}, u32[]{:S(2)}, u32[]{:S(2)}) %collective-permute-start) | collective-permute-done | bytes 262176 | tf_op jit(solution)/shard_map/while/body/eval_jaxpr/ppermute | solution.py:9
  413.8 1.9 collective-permute-start
  415.8 9.6 %collective-permute-done = f32[16,4096]{1,0:T(8,128)S(1)} collective-permute-done((f32[16,4096]{1,0:T(8,128)S(1)}, f32[16,4096]{1,0:T(8,128)S(1)}, u32[]{:S(2)}, u32[]{:S(2)}) %collective-permute-start) | collective-permute-done | bytes 262176 | tf_op jit(solution)/shard_map/while/body/eval_jaxpr/ppermute | solution.py:9
  425.9 1.9 collective-permute-start
  427.8 9.6 %collective-permute-done = f32[16,4096]{1,0:T(8,128)S(1)} collective-permute-done((f32[16,4096]{1,0:T(8,128)S(1)}, f32[16,4096]{1,0:T(8,128)S(1)}, u32[]{:S(2)}, u32[]{:S(2)}) %collective-permute-start) | collective-permute-done | bytes 262176 | tf_op jit(solution)/shard_map/while/body/eval_jaxpr/ppermute | solution.py:9
  438.0 1.9 collective-permute-start
  439.9 9.6 %collective-permute-done = f32[16,4096]{1,0:T(8,128)S(1)} collective-permute-done((f32[16,4096]{1,0:T(8,128)S(1)}, f32[16,4096]{1,0:T(8,128)S(1)}, u32[]{:S(2)}, u32[]{:S(2)}) %collective-permute-start) | collective-permute-done | bytes 262176 | tf_op jit(solution)/shard_map/while/body/eval_jaxpr/ppermute | solution.py:9
  450.0 1.9 collective-permute-start
  452.0 9.6 %collective-permute-done = f32[16,4096]{1,0:T(8,128)S(1)} collective-permute-done((f32[16,4096]{1,0:T(8,128)S(1)}, f32[16,4096]{1,0:T(8,128)S(1)}, u32[]{:S(2)}, u32[]{:S(2)}) %collective-permute-start) | collective-permute-done | bytes 262176 | tf_op jit(solution)/shard_map/while/body/eval_jaxpr/ppermute | solution.py:9
  462.1 1.9 collective-permute-start
  464.1 9.6 %collective-permute-done = f32[16,4096]{1,0:T(8,128)S(1)} collective-permute-done((f32[16,4096]{1,0:T(8,128)S(1)}, f32[16,4096]{1,0:T(8,128)S(1)}, u32[]{:S(2)}, u32[]{:S(2)}) %collective-permute-start) | collective-permute-done | bytes 262176 | tf_op jit(solution)/shard_map/while/body/eval_jaxpr/ppermute | solution.py:9
  476.1 9.6 %collective-permute-done = f32[16,4096]{1,0:T(8,128)S(1)} collective-permute-done((f32[16,4096]{1,0:T(8,128)S(1)}, f32[16,4096]{1,0:T(8,128)S(1)}, u32[]{:S(2)}, u32[]{:S(2)}) %collective-permute-start) | collective-permute-done | bytes 262176 | tf_op jit(solution)/shard_map/while/body/eval_jaxpr/ppermute | solution.py:9
  488.2 9.6 %collective-permute-done = f32[16,4096]{1,0:T(8,128)S(1)} collective-permute-done((f32[16,4096]{1,0:T(8,128)S(1)}, f32[16,4096]{1,0:T(8,128)S(1)}, u32[]{:S(2)}, u32[]{:S(2)}) %collective-permute-start) | collective-permute-done | bytes 262176 | tf_op jit(solution)/shard_map/while/body/eval_jaxpr/ppermute | solution.py:9
  (73 shorter events, 40.8 us)
Async XLA Ops:
  7.2 22.0 %copy-start = (bf16[1,16,4096]{2,1,0:T(8,128)(2,1)S(1)}, bf16[1,16,4096]{2,1,0:T(8,128)(2,1)}, u32[]{:S(2)}) copy-start(bf16[1,16,4096]{2,1,0:T(8,128)(2,1)} %param.10) | copy-start | bytes 393220
  7.2 62.9 %copy-start.1 = (bf16[1,256,4096]{2,1,0:T(8,128)(2,1)S(1)}, bf16[1,256,4096]{2,1,0:T(8,128)(2,1)}, u32[]{:S(2)}) copy-start(bf16[1,256,4096]{2,1,0:T(8,128)(2,1)} %param.7) | copy-start | bytes 6291460
  7.2 83.7 %all-gather.3.cloned.1.call-start = ((), (), s32[]{:S(2)}) async-start(), calls=%async_computation.3 | async-start | bytes 4325376 | tf_op jit(solution)/shard_map/all_gather | solution.py:54
  11.0 31.5 %all-to-all-start = ((bf16[16,1,2]{2,1,0:T(2,128)(2,1)}), bf16[16,1,2]{2,1,0:T(2,128)(2,1)S(1)}, u32[]{:S(2)}, u32[]{:S(2)}) async-start(bf16[16,1,2]{2,1,0:T(2,128)(2,1)} %all_to_all.16), calls=%async_computation | async-start | bytes 16384 | tf_op jit(solution)/shard_map/all_to_all | solution.py:41
  42.5 27.5 %all-to-all-start.1 = ((bf16[16,2,4096]{2,1,0:T(2,128)(2,1)}), bf16[16,2,4096]{2,1,0:T(2,128)(2,1)S(1)}, u32[]{:S(2)}, u32[]{:S(2)}) async-start(bf16[16,2,4096]{2,1,0:T(2,128)(2,1)} %reshape.99), calls=%async_computation.1 | async-start | bytes 524288 | tf_op jit(solution)/shard_map/all_to_all | solution.py:40
  70.8 23.8 %copy-start.3 = (s32[1,256]{1,0:T(1,128)S(1)}, s32[1,256]{1,0:T(1,128)}, u32[]{:S(2)}) copy-start(s32[1,256]{1,0:T(1,128)} %param.9) | copy-start | bytes 3076
  90.9 5.3 %copy-start.2 = (bf16[1,512,4096]{2,1,0:T(8,128)(2,1)S(1)}, bf16[1,512,4096]{2,1,0:T(8,128)(2,1)}, u32[]{:S(2)}) copy-start(bf16[1,512,4096]{2,1,0:T(8,128)(2,1)} %all-gather.3.cloned.1.call-done) | copy-start | bytes 12582916
  104.2 394.8 %all-to-all-start.2 = ((bf16[16,2,4096]{2,1,0:T(2,128)(2,1)}), bf16[16,2,4096]{2,1,0:T(2,128)(2,1)S(1)}, u32[]{:S(2)}, u32[]{:S(2)}) async-start(bf16[16,2,4096]{2,1,0:T(2,128)(2,1)} %reshape.101), calls=%async_computation.2 | async-start | bytes 524288 | tf_op jit(solution)/shard_map/all_to_all | solution.py:94
  120.4 14.9 %collective-permute-start = (f32[16,4096]{1,0:T(8,128)S(1)}, f32[16,4096]{1,0:T(8,128)S(1)}, u32[]{:S(2)}, u32[]{:S(2)}) collective-permute-start(f32[16,4096]{1,0:T(8,128)S(1)} %get-tuple-element.201), channel_id=1, source_target_pairs={{0,16},{16,32},{32,48},{48,64},{64,80},{80,96},{96,112},{112,128},... | collective-permute-start | bytes 786440 | tf_op jit(solution)/shard_map/while/body/eval_jaxpr/ppermute | solution.py:9
  135.7 11.9 %collective-permute-start = (f32[16,4096]{1,0:T(8,128)S(1)}, f32[16,4096]{1,0:T(8,128)S(1)}, u32[]{:S(2)}, u32[]{:S(2)}) collective-permute-start(f32[16,4096]{1,0:T(8,128)S(1)} %get-tuple-element.201), channel_id=1, source_target_pairs={{0,16},{16,32},{32,48},{48,64},{64,80},{80,96},{96,112},{112,128},... | collective-permute-start | bytes 786440 | tf_op jit(solution)/shard_map/while/body/eval_jaxpr/ppermute | solution.py:9
  148.2 11.6 %collective-permute-start = (f32[16,4096]{1,0:T(8,128)S(1)}, f32[16,4096]{1,0:T(8,128)S(1)}, u32[]{:S(2)}, u32[]{:S(2)}) collective-permute-start(f32[16,4096]{1,0:T(8,128)S(1)} %get-tuple-element.201), channel_id=1, source_target_pairs={{0,16},{16,32},{32,48},{48,64},{64,80},{80,96},{96,112},{112,128},... | collective-permute-start | bytes 786440 | tf_op jit(solution)/shard_map/while/body/eval_jaxpr/ppermute | solution.py:9
  160.2 11.6 %collective-permute-start = (f32[16,4096]{1,0:T(8,128)S(1)}, f32[16,4096]{1,0:T(8,128)S(1)}, u32[]{:S(2)}, u32[]{:S(2)}) collective-permute-start(f32[16,4096]{1,0:T(8,128)S(1)} %get-tuple-element.201), channel_id=1, source_target_pairs={{0,16},{16,32},{32,48},{48,64},{64,80},{80,96},{96,112},{112,128},... | collective-permute-start | bytes 786440 | tf_op jit(solution)/shard_map/while/body/eval_jaxpr/ppermute | solution.py:9
  172.3 11.6 %collective-permute-start = (f32[16,4096]{1,0:T(8,128)S(1)}, f32[16,4096]{1,0:T(8,128)S(1)}, u32[]{:S(2)}, u32[]{:S(2)}) collective-permute-start(f32[16,4096]{1,0:T(8,128)S(1)} %get-tuple-element.201), channel_id=1, source_target_pairs={{0,16},{16,32},{32,48},{48,64},{64,80},{80,96},{96,112},{112,128},... | collective-permute-start | bytes 786440 | tf_op jit(solution)/shard_map/while/body/eval_jaxpr/ppermute | solution.py:9
  184.4 11.6 %collective-permute-start = (f32[16,4096]{1,0:T(8,128)S(1)}, f32[16,4096]{1,0:T(8,128)S(1)}, u32[]{:S(2)}, u32[]{:S(2)}) collective-permute-start(f32[16,4096]{1,0:T(8,128)S(1)} %get-tuple-element.201), channel_id=1, source_target_pairs={{0,16},{16,32},{32,48},{48,64},{64,80},{80,96},{96,112},{112,128},... | collective-permute-start | bytes 786440 | tf_op jit(solution)/shard_map/while/body/eval_jaxpr/ppermute | solution.py:9
  196.5 11.6 %collective-permute-start = (f32[16,4096]{1,0:T(8,128)S(1)}, f32[16,4096]{1,0:T(8,128)S(1)}, u32[]{:S(2)}, u32[]{:S(2)}) collective-permute-start(f32[16,4096]{1,0:T(8,128)S(1)} %get-tuple-element.201), channel_id=1, source_target_pairs={{0,16},{16,32},{32,48},{48,64},{64,80},{80,96},{96,112},{112,128},... | collective-permute-start | bytes 786440 | tf_op jit(solution)/shard_map/while/body/eval_jaxpr/ppermute | solution.py:9
  208.5 11.6 %collective-permute-start = (f32[16,4096]{1,0:T(8,128)S(1)}, f32[16,4096]{1,0:T(8,128)S(1)}, u32[]{:S(2)}, u32[]{:S(2)}) collective-permute-start(f32[16,4096]{1,0:T(8,128)S(1)} %get-tuple-element.201), channel_id=1, source_target_pairs={{0,16},{16,32},{32,48},{48,64},{64,80},{80,96},{96,112},{112,128},... | collective-permute-start | bytes 786440 | tf_op jit(solution)/shard_map/while/body/eval_jaxpr/ppermute | solution.py:9
  220.6 11.6 %collective-permute-start = (f32[16,4096]{1,0:T(8,128)S(1)}, f32[16,4096]{1,0:T(8,128)S(1)}, u32[]{:S(2)}, u32[]{:S(2)}) collective-permute-start(f32[16,4096]{1,0:T(8,128)S(1)} %get-tuple-element.201), channel_id=1, source_target_pairs={{0,16},{16,32},{32,48},{48,64},{64,80},{80,96},{96,112},{112,128},... | collective-permute-start | bytes 786440 | tf_op jit(solution)/shard_map/while/body/eval_jaxpr/ppermute | solution.py:9
  232.7 11.6 %collective-permute-start = (f32[16,4096]{1,0:T(8,128)S(1)}, f32[16,4096]{1,0:T(8,128)S(1)}, u32[]{:S(2)}, u32[]{:S(2)}) collective-permute-start(f32[16,4096]{1,0:T(8,128)S(1)} %get-tuple-element.201), channel_id=1, source_target_pairs={{0,16},{16,32},{32,48},{48,64},{64,80},{80,96},{96,112},{112,128},... | collective-permute-start | bytes 786440 | tf_op jit(solution)/shard_map/while/body/eval_jaxpr/ppermute | solution.py:9
  244.8 11.6 %collective-permute-start = (f32[16,4096]{1,0:T(8,128)S(1)}, f32[16,4096]{1,0:T(8,128)S(1)}, u32[]{:S(2)}, u32[]{:S(2)}) collective-permute-start(f32[16,4096]{1,0:T(8,128)S(1)} %get-tuple-element.201), channel_id=1, source_target_pairs={{0,16},{16,32},{32,48},{48,64},{64,80},{80,96},{96,112},{112,128},... | collective-permute-start | bytes 786440 | tf_op jit(solution)/shard_map/while/body/eval_jaxpr/ppermute | solution.py:9
  256.8 11.6 %collective-permute-start = (f32[16,4096]{1,0:T(8,128)S(1)}, f32[16,4096]{1,0:T(8,128)S(1)}, u32[]{:S(2)}, u32[]{:S(2)}) collective-permute-start(f32[16,4096]{1,0:T(8,128)S(1)} %get-tuple-element.201), channel_id=1, source_target_pairs={{0,16},{16,32},{32,48},{48,64},{64,80},{80,96},{96,112},{112,128},... | collective-permute-start | bytes 786440 | tf_op jit(solution)/shard_map/while/body/eval_jaxpr/ppermute | solution.py:9
  268.9 11.6 %collective-permute-start = (f32[16,4096]{1,0:T(8,128)S(1)}, f32[16,4096]{1,0:T(8,128)S(1)}, u32[]{:S(2)}, u32[]{:S(2)}) collective-permute-start(f32[16,4096]{1,0:T(8,128)S(1)} %get-tuple-element.201), channel_id=1, source_target_pairs={{0,16},{16,32},{32,48},{48,64},{64,80},{80,96},{96,112},{112,128},... | collective-permute-start | bytes 786440 | tf_op jit(solution)/shard_map/while/body/eval_jaxpr/ppermute | solution.py:9
  281.0 11.6 %collective-permute-start = (f32[16,4096]{1,0:T(8,128)S(1)}, f32[16,4096]{1,0:T(8,128)S(1)}, u32[]{:S(2)}, u32[]{:S(2)}) collective-permute-start(f32[16,4096]{1,0:T(8,128)S(1)} %get-tuple-element.201), channel_id=1, source_target_pairs={{0,16},{16,32},{32,48},{48,64},{64,80},{80,96},{96,112},{112,128},... | collective-permute-start | bytes 786440 | tf_op jit(solution)/shard_map/while/body/eval_jaxpr/ppermute | solution.py:9
  293.1 11.6 %collective-permute-start = (f32[16,4096]{1,0:T(8,128)S(1)}, f32[16,4096]{1,0:T(8,128)S(1)}, u32[]{:S(2)}, u32[]{:S(2)}) collective-permute-start(f32[16,4096]{1,0:T(8,128)S(1)} %get-tuple-element.201), channel_id=1, source_target_pairs={{0,16},{16,32},{32,48},{48,64},{64,80},{80,96},{96,112},{112,128},... | collective-permute-start | bytes 786440 | tf_op jit(solution)/shard_map/while/body/eval_jaxpr/ppermute | solution.py:9
  305.1 11.6 %collective-permute-start = (f32[16,4096]{1,0:T(8,128)S(1)}, f32[16,4096]{1,0:T(8,128)S(1)}, u32[]{:S(2)}, u32[]{:S(2)}) collective-permute-start(f32[16,4096]{1,0:T(8,128)S(1)} %get-tuple-element.201), channel_id=1, source_target_pairs={{0,16},{16,32},{32,48},{48,64},{64,80},{80,96},{96,112},{112,128},... | collective-permute-start | bytes 786440 | tf_op jit(solution)/shard_map/while/body/eval_jaxpr/ppermute | solution.py:9
  317.2 11.6 %collective-permute-start = (f32[16,4096]{1,0:T(8,128)S(1)}, f32[16,4096]{1,0:T(8,128)S(1)}, u32[]{:S(2)}, u32[]{:S(2)}) collective-permute-start(f32[16,4096]{1,0:T(8,128)S(1)} %get-tuple-element.201), channel_id=1, source_target_pairs={{0,16},{16,32},{32,48},{48,64},{64,80},{80,96},{96,112},{112,128},... | collective-permute-start | bytes 786440 | tf_op jit(solution)/shard_map/while/body/eval_jaxpr/ppermute | solution.py:9
  329.3 11.6 %collective-permute-start = (f32[16,4096]{1,0:T(8,128)S(1)}, f32[16,4096]{1,0:T(8,128)S(1)}, u32[]{:S(2)}, u32[]{:S(2)}) collective-permute-start(f32[16,4096]{1,0:T(8,128)S(1)} %get-tuple-element.201), channel_id=1, source_target_pairs={{0,16},{16,32},{32,48},{48,64},{64,80},{80,96},{96,112},{112,128},... | collective-permute-start | bytes 786440 | tf_op jit(solution)/shard_map/while/body/eval_jaxpr/ppermute | solution.py:9
  341.4 11.6 %collective-permute-start = (f32[16,4096]{1,0:T(8,128)S(1)}, f32[16,4096]{1,0:T(8,128)S(1)}, u32[]{:S(2)}, u32[]{:S(2)}) collective-permute-start(f32[16,4096]{1,0:T(8,128)S(1)} %get-tuple-element.201), channel_id=1, source_target_pairs={{0,16},{16,32},{32,48},{48,64},{64,80},{80,96},{96,112},{112,128},... | collective-permute-start | bytes 786440 | tf_op jit(solution)/shard_map/while/body/eval_jaxpr/ppermute | solution.py:9
  353.4 11.6 %collective-permute-start = (f32[16,4096]{1,0:T(8,128)S(1)}, f32[16,4096]{1,0:T(8,128)S(1)}, u32[]{:S(2)}, u32[]{:S(2)}) collective-permute-start(f32[16,4096]{1,0:T(8,128)S(1)} %get-tuple-element.201), channel_id=1, source_target_pairs={{0,16},{16,32},{32,48},{48,64},{64,80},{80,96},{96,112},{112,128},... | collective-permute-start | bytes 786440 | tf_op jit(solution)/shard_map/while/body/eval_jaxpr/ppermute | solution.py:9
  365.5 11.6 %collective-permute-start = (f32[16,4096]{1,0:T(8,128)S(1)}, f32[16,4096]{1,0:T(8,128)S(1)}, u32[]{:S(2)}, u32[]{:S(2)}) collective-permute-start(f32[16,4096]{1,0:T(8,128)S(1)} %get-tuple-element.201), channel_id=1, source_target_pairs={{0,16},{16,32},{32,48},{48,64},{64,80},{80,96},{96,112},{112,128},... | collective-permute-start | bytes 786440 | tf_op jit(solution)/shard_map/while/body/eval_jaxpr/ppermute | solution.py:9
  377.6 11.6 %collective-permute-start = (f32[16,4096]{1,0:T(8,128)S(1)}, f32[16,4096]{1,0:T(8,128)S(1)}, u32[]{:S(2)}, u32[]{:S(2)}) collective-permute-start(f32[16,4096]{1,0:T(8,128)S(1)} %get-tuple-element.201), channel_id=1, source_target_pairs={{0,16},{16,32},{32,48},{48,64},{64,80},{80,96},{96,112},{112,128},... | collective-permute-start | bytes 786440 | tf_op jit(solution)/shard_map/while/body/eval_jaxpr/ppermute | solution.py:9
  389.7 11.6 %collective-permute-start = (f32[16,4096]{1,0:T(8,128)S(1)}, f32[16,4096]{1,0:T(8,128)S(1)}, u32[]{:S(2)}, u32[]{:S(2)}) collective-permute-start(f32[16,4096]{1,0:T(8,128)S(1)} %get-tuple-element.201), channel_id=1, source_target_pairs={{0,16},{16,32},{32,48},{48,64},{64,80},{80,96},{96,112},{112,128},... | collective-permute-start | bytes 786440 | tf_op jit(solution)/shard_map/while/body/eval_jaxpr/ppermute | solution.py:9
  401.7 11.6 %collective-permute-start = (f32[16,4096]{1,0:T(8,128)S(1)}, f32[16,4096]{1,0:T(8,128)S(1)}, u32[]{:S(2)}, u32[]{:S(2)}) collective-permute-start(f32[16,4096]{1,0:T(8,128)S(1)} %get-tuple-element.201), channel_id=1, source_target_pairs={{0,16},{16,32},{32,48},{48,64},{64,80},{80,96},{96,112},{112,128},... | collective-permute-start | bytes 786440 | tf_op jit(solution)/shard_map/while/body/eval_jaxpr/ppermute | solution.py:9
  413.8 11.6 %collective-permute-start = (f32[16,4096]{1,0:T(8,128)S(1)}, f32[16,4096]{1,0:T(8,128)S(1)}, u32[]{:S(2)}, u32[]{:S(2)}) collective-permute-start(f32[16,4096]{1,0:T(8,128)S(1)} %get-tuple-element.201), channel_id=1, source_target_pairs={{0,16},{16,32},{32,48},{48,64},{64,80},{80,96},{96,112},{112,128},... | collective-permute-start | bytes 786440 | tf_op jit(solution)/shard_map/while/body/eval_jaxpr/ppermute | solution.py:9
  425.9 11.6 %collective-permute-start = (f32[16,4096]{1,0:T(8,128)S(1)}, f32[16,4096]{1,0:T(8,128)S(1)}, u32[]{:S(2)}, u32[]{:S(2)}) collective-permute-start(f32[16,4096]{1,0:T(8,128)S(1)} %get-tuple-element.201), channel_id=1, source_target_pairs={{0,16},{16,32},{32,48},{48,64},{64,80},{80,96},{96,112},{112,128},... | collective-permute-start | bytes 786440 | tf_op jit(solution)/shard_map/while/body/eval_jaxpr/ppermute | solution.py:9
  438.0 11.6 %collective-permute-start = (f32[16,4096]{1,0:T(8,128)S(1)}, f32[16,4096]{1,0:T(8,128)S(1)}, u32[]{:S(2)}, u32[]{:S(2)}) collective-permute-start(f32[16,4096]{1,0:T(8,128)S(1)} %get-tuple-element.201), channel_id=1, source_target_pairs={{0,16},{16,32},{32,48},{48,64},{64,80},{80,96},{96,112},{112,128},... | collective-permute-start | bytes 786440 | tf_op jit(solution)/shard_map/while/body/eval_jaxpr/ppermute | solution.py:9
  450.0 11.6 %collective-permute-start = (f32[16,4096]{1,0:T(8,128)S(1)}, f32[16,4096]{1,0:T(8,128)S(1)}, u32[]{:S(2)}, u32[]{:S(2)}) collective-permute-start(f32[16,4096]{1,0:T(8,128)S(1)} %get-tuple-element.201), channel_id=1, source_target_pairs={{0,16},{16,32},{32,48},{48,64},{64,80},{80,96},{96,112},{112,128},... | collective-permute-start | bytes 786440 | tf_op jit(solution)/shard_map/while/body/eval_jaxpr/ppermute | solution.py:9
  462.1 11.6 %collective-permute-start = (f32[16,4096]{1,0:T(8,128)S(1)}, f32[16,4096]{1,0:T(8,128)S(1)}, u32[]{:S(2)}, u32[]{:S(2)}) collective-permute-start(f32[16,4096]{1,0:T(8,128)S(1)} %get-tuple-element.201), channel_id=1, source_target_pairs={{0,16},{16,32},{32,48},{48,64},{64,80},{80,96},{96,112},{112,128},... | collective-permute-start | bytes 786440 | tf_op jit(solution)/shard_map/while/body/eval_jaxpr/ppermute | solution.py:9
  474.2 11.6 %collective-permute-start = (f32[16,4096]{1,0:T(8,128)S(1)}, f32[16,4096]{1,0:T(8,128)S(1)}, u32[]{:S(2)}, u32[]{:S(2)}) collective-permute-start(f32[16,4096]{1,0:T(8,128)S(1)} %get-tuple-element.201), channel_id=1, source_target_pairs={{0,16},{16,32},{32,48},{48,64},{64,80},{80,96},{96,112},{112,128},... | collective-permute-start | bytes 786440 | tf_op jit(solution)/shard_map/while/body/eval_jaxpr/ppermute | solution.py:9
  486.3 11.6 %collective-permute-start = (f32[16,4096]{1,0:T(8,128)S(1)}, f32[16,4096]{1,0:T(8,128)S(1)}, u32[]{:S(2)}, u32[]{:S(2)}) collective-permute-start(f32[16,4096]{1,0:T(8,128)S(1)} %get-tuple-element.201), channel_id=1, source_target_pairs={{0,16},{16,32},{32,48},{48,64},{64,80},{80,96},{96,112},{112,128},... | collective-permute-start | bytes 786440 | tf_op jit(solution)/shard_map/while/body/eval_jaxpr/ppermute | solution.py:9
Sparse Core Ops, SparseCore 0:
  10.2 80.6 all-gather.2
where the time goes:
time: 509 us; the launch traced here: 507 us
  waiting for transfers between devices  358 us (70%)
  starting transfers between devices  98.1 us (19%)
  matrix products  28.6 us (6%)
  between operations  14.1 us (3%)
    ppermute x31, waiting for transfers between devices, from_behind(): return lax.ppermute(x, axis, [(i, (i + by) % count) for i in range(count)])  303 us
    ppermute x31, starting transfers between devices, from_behind(): return lax.ppermute(x, axis, [(i, (i + by) % count) for i in range(count)])  59.4 us
    all_to_all x1, waiting for transfers between devices, body(): lax.all_to_all(packed, 'group', split_axis=0, concat_axis=0, tiled=True)  22.5 us
    all_gather x1, waiting for transfers between devices, body(): gathered = lax.all_gather(own_passages, 'blk', axis=0, tiled=True)  20 us
    all_to_all x1, starting transfers between devices, body(): lax.all_to_all(live_flags, 'group', split_axis=0, concat_axis=0, tiled=True)  18.2 us
    all_to_all x1, starting transfers between devices, body(): lax.all_to_all(slot_grads, 'group', split_axis=0, concat_axis=0, tiled=True)  15.7 us
    dot_general x32, matrix products, contrib(): jnp.einsum('qp,qd->pd', coef_cols, query_rows, preferred_element_type=jnp...  15.3 us
    all_to_all x1, waiting for transfers between devices, body(): lax.all_to_all(live_flags, 'group', split_axis=0, concat_axis=0, tiled=True)  12.1 us
  transfers between devices with their start and end apart: 35, of which 34 were waited for; matrix products, arithmetic and copies ran while one was open for 4% of the time, Pallas kernels for 0%

commit v1 on v0

--- a/solution.py
+++ b/solution.py
@@ -51,7 +51,16 @@
     target_hot = (targets[:, None] == jnp.arange(total_rows, dtype=jnp.int32)[None, :]).astype(
         jnp.float32
     )
-    gathered = lax.all_gather(own_passages, "blk", axis=0, tiled=True)
+
+    def store_area(z, along_axis):
+        return jnp.concatenate(
+            lax.all_to_all(
+                jnp.stack([z for _ in range(lax.axis_size(along_axis))], 0), along_axis, 0, 0
+            ),
+            0,
+        )
+
+    gathered = store_area(own_passages, "blk")
     in_scores = score_multiplier * jnp.einsum(
         "qd,pd->qp", query_rows, gathered, preferred_element_type=jnp.float32
     )

time: 509 us -> 568 us (1.12)
  waiting for transfers between devices: 358 us -> 410 us
  blocking collectives: 0 us -> 21.3 us
  between operations: 14.1 us -> 0.75 us
    all_to_all x1, waiting for transfers between devices: 22.5 us -> 92.8 us  [store_area(): lax.all_to_all(jnp.stack([z for _ in range(lax.axis_size(along_axis))], 0...]
    all_to_all x0 -> x1, blocking collectives: none -> 21.3 us  [body(): lax.all_to_all(packed, 'group', split_axis=0, concat_axis=0, tiled=True)]
    all_gather x1 -> x0, waiting for transfers between devices: 20 us -> none  [body(): gathered = lax.all_gather(own_passages, 'blk', axis=0, tiled=True)]
    all_to_all x1, starting transfers between devices: 15.7 us -> 6.41 us  [body(): lax.all_to_all(slot_grads, 'group', split_axis=0, concat_axis=0, tiled=True)]
  transfers between devices with their start and end apart: 35 -> 34, of which waited for: 34 -> 33; matrix products, arithmetic and copies ran while one was open for 4% -> 3% of each run, Pallas kernels for 0% -> 0%
where the time goes in v1:
time: 568 us; the launch traced here: 566 us
  waiting for transfers between devices  410 us (72%)
  starting transfers between devices  92.6 us (16%)
  matrix products  30.3 us (5%)
  blocking collectives  21.3 us (4%)
    ppermute x31, waiting for transfers between devices, from_behind(): return lax.ppermute(x, axis, [(i, (i + by) % count) for i in range(count)])  305 us
    all_to_all x1, waiting for transfers between devices, store_area(): lax.all_to_all(jnp.stack([z for _ in range(lax.axis_size(along_axis))], 0...  92.8 us
    ppermute x31, starting transfers between devices, from_behind(): return lax.ppermute(x, axis, [(i, (i + by) % count) for i in range(count)])  59.4 us
    all_to_all x1, blocking collectives, body(): lax.all_to_all(packed, 'group', split_axis=0, concat_axis=0, tiled=True)  21.3 us
    all_to_all x1, starting transfers between devices, body(): lax.all_to_all(live_flags, 'group', split_axis=0, concat_axis=0, tiled=True)  18.2 us
    dot_general x32, matrix products, contrib(): jnp.einsum('qp,qd->pd', coef_cols, query_rows, preferred_element_type=jnp...  15.3 us
    all_to_all x1, waiting for transfers between devices, body(): lax.all_to_all(live_flags, 'group', split_axis=0, concat_axis=0, tiled=True)  12.8 us
  transfers between devices with their start and end apart: 34, of which 33 were waited for; matrix products, arithmetic and copies ran while one was open for 3% of the time, Pallas kernels for 0%

profile of v1, /device:TPU:8, one launch (start us, length us, event | category | flops | bytes accessed | tf_op | source)
XLA Modules:
  0.0 565.9 jit_solution(3636467826412425699)
XLA Ops:
  3.7 18.2 %all-to-all-start.1 = ((bf16[16,1,2]{2,1,0:T(2,128)(2,1)}), bf16[16,1,2]{2,1,0:T(2,128)(2,1)S(1)}, u32[]{:S(2)}, u32[]{:S(2)}) async-start(bf16[16,1,2]{2,1,0:T(2,128)(2,1)} %all_to_all.20), calls=%async_computation.1 | async-start | bytes 16384 | tf_op jit(solution)/shard_map/all_to_all | solution.py:41
  22.5 12.8 %all-to-all-done.1 = bf16[16,1,2]{2,1,0:T(2,128)(2,1)S(1)} async-done(((bf16[16,1,2]{2,1,0:T(2,128)(2,1)}), bf16[16,1,2]{2,1,0:T(2,128)(2,1)S(1)}, u32[]{:S(2)}, u32[]{:S(2)}) %all-to-all-start.1) | async-done | bytes 96 | tf_op jit(solution)/shard_map/all_to_all | solution.py:41
  35.3 21.3 %all_to_all.25 = bf16[16,2,4096]{2,1,0:T(2,128)(2,1)S(1)} all-to-all(bf16[16,2,4096]{2,1,0:T(2,128)(2,1)S(1)} %reshape.104), channel_id=1, replica_groups=mesh['blk'=32,'group'=16] {'group'}, dimensions={0} | all-to-all | bytes 524288 | tf_op jit(solution)/shard_map/all_to_all | solution.py:40
  56.6 3.4 stack.3
  59.9 8.6 %all-to-all-start = ((bf16[32,16,4096]{2,1,0:T(8,128)(2,1)}), bf16[32,16,4096]{2,1,0:T(8,128)(2,1)}, u32[]{:S(2)}, u32[]{:S(2)}) async-start(bf16[32,16,4096]{2,1,0:T(8,128)(2,1)} %stack.3), calls=%async_computation | async-start | bytes 8388608 | tf_op jit(solution)/shard_map/all_to_all | solution.py:57
  69.6 92.8 %all-to-all-done = bf16[32,16,4096]{2,1,0:T(8,128)(2,1)} async-done(((bf16[32,16,4096]{2,1,0:T(8,128)(2,1)}), bf16[32,16,4096]{2,1,0:T(8,128)(2,1)}, u32[]{:S(2)}, u32[]{:S(2)}) %all-to-all-start) | async-done | bytes 4194336 | tf_op jit(solution)/shard_map/all_to_all | solution.py:57
  162.5 3.6 fusion.31
  167.0 5.6 fusion.9
  173.2 3.3 fusion.4
  177.4 6.4 %all-to-all-start.3 = ((bf16[16,2,4096]{2,1,0:T(2,128)(2,1)}), bf16[16,2,4096]{2,1,0:T(2,128)(2,1)S(1)}, u32[]{:S(2)}, u32[]{:S(2)}) async-start(bf16[16,2,4096]{2,1,0:T(2,128)(2,1)} %reshape.106), calls=%async_computation.3 | async-start | bytes 524288 | tf_op jit(solution)/shard_map/all_to_all | solution.py:103
  184.3 379.9 %while.15 = (s32[]{:T(128)}, f32[16,4096]{1,0:T(8,128)S(1)}, s32[]{:T(128)}, bf16[256,512]{1,0:T(8,128)(2,1)S(1)}, bf16[256,4096]{1,0:T(8,128)(2,1)S(1)}, /*inde...) while((s32[]{:T(128)}, f32[16,4096]{1,0:T(8,128)S(1)}, ...), condition=%wide.region_9.10_spmd, body=%wide.region_8.9_spmd.sunk | while | flops 33619984 | bytes 3735892 | solution.py:93
  184.3 1.9 collective-permute-start
  186.3 15.2 %collective-permute-done = f32[16,4096]{1,0:T(8,128)S(1)} collective-permute-done((f32[16,4096]{1,0:T(8,128)S(1)}, f32[16,4096]{1,0:T(8,128)S(1)}, u32[]{:S(2)}, u32[]{:S(2)}) %collective-permute-start) | collective-permute-done | bytes 262176 | tf_op jit(solution)/shard_map/while/body/eval_jaxpr/ppermute | solution.py:9
  202.0 1.9 collective-permute-start
  203.9 9.6 %collective-permute-done = f32[16,4096]{1,0:T(8,128)S(1)} collective-permute-done((f32[16,4096]{1,0:T(8,128)S(1)}, f32[16,4096]{1,0:T(8,128)S(1)}, u32[]{:S(2)}, u32[]{:S(2)}) %collective-permute-start) | collective-permute-done | bytes 262176 | tf_op jit(solution)/shard_map/while/body/eval_jaxpr/ppermute | solution.py:9
  214.1 1.9 collective-permute-start
  216.0 9.6 %collective-permute-done = f32[16,4096]{1,0:T(8,128)S(1)} collective-permute-done((f32[16,4096]{1,0:T(8,128)S(1)}, f32[16,4096]{1,0:T(8,128)S(1)}, u32[]{:S(2)}, u32[]{:S(2)}) %collective-permute-start) | collective-permute-done | bytes 262176 | tf_op jit(solution)/shard_map/while/body/eval_jaxpr/ppermute | solution.py:9
  226.1 1.9 collective-permute-start
  228.1 9.6 %collective-permute-done = f32[16,4096]{1,0:T(8,128)S(1)} collective-permute-done((f32[16,4096]{1,0:T(8,128)S(1)}, f32[16,4096]{1,0:T(8,128)S(1)}, u32[]{:S(2)}, u32[]{:S(2)}) %collective-permute-start) | collective-permute-done | bytes 262176 | tf_op jit(solution)/shard_map/while/body/eval_jaxpr/ppermute | solution.py:9
  240.2 9.6 %collective-permute-done = f32[16,4096]{1,0:T(8,128)S(1)} collective-permute-done((f32[16,4096]{1,0:T(8,128)S(1)}, f32[16,4096]{1,0:T(8,128)S(1)}, u32[]{:S(2)}, u32[]{:S(2)}) %collective-permute-start) | collective-permute-done | bytes 262176 | tf_op jit(solution)/shard_map/while/body/eval_jaxpr/ppermute | solution.py:9
  252.2 9.6 %collective-permute-done = f32[16,4096]{1,0:T(8,128)S(1)} collective-permute-done((f32[16,4096]{1,0:T(8,128)S(1)}, f32[16,4096]{1,0:T(8,128)S(1)}, u32[]{:S(2)}, u32[]{:S(2)}) %collective-permute-start) | collective-permute-done | bytes 262176 | tf_op jit(solution)/shard_map/while/body/eval_jaxpr/ppermute | solution.py:9
  262.4 1.9 collective-permute-start
  264.3 9.6 %collective-permute-done = f32[16,4096]{1,0:T(8,128)S(1)} collective-permute-done((f32[16,4096]{1,0:T(8,128)S(1)}, f32[16,4096]{1,0:T(8,128)S(1)}, u32[]{:S(2)}, u32[]{:S(2)}) %collective-permute-start) | collective-permute-done | bytes 262176 | tf_op jit(solution)/shard_map/while/body/eval_jaxpr/ppermute | solution.py:9
  274.4 1.9 collective-permute-start
  276.4 9.6 %collective-permute-done = f32[16,4096]{1,0:T(8,128)S(1)} collective-permute-done((f32[16,4096]{1,0:T(8,128)S(1)}, f32[16,4096]{1,0:T(8,128)S(1)}, u32[]{:S(2)}, u32[]{:S(2)}) %collective-permute-start) | collective-permute-done | bytes 262176 | tf_op jit(solution)/shard_map/while/body/eval_jaxpr/ppermute | solution.py:9
  286.5 1.9 collective-permute-start
  288.5 9.6 %collective-permute-done = f32[16,4096]{1,0:T(8,128)S(1)} collective-permute-done((f32[16,4096]{1,0:T(8,128)S(1)}, f32[16,4096]{1,0:T(8,128)S(1)}, u32[]{:S(2)}, u32[]{:S(2)}) %collective-permute-start) | collective-permute-done | bytes 262176 | tf_op jit(solution)/shard_map/while/body/eval_jaxpr/ppermute | solution.py:9
  298.6 1.9 collective-permute-start
  300.5 9.6 %collective-permute-done = f32[16,4096]{1,0:T(8,128)S(1)} collective-permute-done((f32[16,4096]{1,0:T(8,128)S(1)}, f32[16,4096]{1,0:T(8,128)S(1)}, u32[]{:S(2)}, u32[]{:S(2)}) %collective-permute-start) | collective-permute-done | bytes 262176 | tf_op jit(solution)/shard_map/while/body/eval_jaxpr/ppermute | solution.py:9
  310.7 1.9 collective-permute-start
  312.6 9.6 %collective-permute-done = f32[16,4096]{1,0:T(8,128)S(1)} collective-permute-done((f32[16,4096]{1,0:T(8,128)S(1)}, f32[16,4096]{1,0:T(8,128)S(1)}, u32[]{:S(2)}, u32[]{:S(2)}) %collective-permute-start) | collective-permute-done | bytes 262176 | tf_op jit(solution)/shard_map/while/body/eval_jaxpr/ppermute | solution.py:9
  324.7 9.6 %collective-permute-done = f32[16,4096]{1,0:T(8,128)S(1)} collective-permute-done((f32[16,4096]{1,0:T(8,128)S(1)}, f32[16,4096]{1,0:T(8,128)S(1)}, u32[]{:S(2)}, u32[]{:S(2)}) %collective-permute-start) | collective-permute-done | bytes 262176 | tf_op jit(solution)/shard_map/while/body/eval_jaxpr/ppermute | solution.py:9
  334.8 1.9 collective-permute-start
  336.8 9.6 %collective-permute-done = f32[16,4096]{1,0:T(8,128)S(1)} collective-permute-done((f32[16,4096]{1,0:T(8,128)S(1)}, f32[16,4096]{1,0:T(8,128)S(1)}, u32[]{:S(2)}, u32[]{:S(2)}) %collective-permute-start) | collective-permute-done | bytes 262176 | tf_op jit(solution)/shard_map/while/body/eval_jaxpr/ppermute | solution.py:9
  346.9 1.9 collective-permute-start
  348.8 9.6 %collective-permute-done = f32[16,4096]{1,0:T(8,128)S(1)} collective-permute-done((f32[16,4096]{1,0:T(8,128)S(1)}, f32[16,4096]{1,0:T(8,128)S(1)}, u32[]{:S(2)}, u32[]{:S(2)}) %collective-permute-start) | collective-permute-done | bytes 262176 | tf_op jit(solution)/shard_map/while/body/eval_jaxpr/ppermute | solution.py:9
  359.0 1.9 collective-permute-start
  360.9 9.6 %collective-permute-done = f32[16,4096]{1,0:T(8,128)S(1)} collective-permute-done((f32[16,4096]{1,0:T(8,128)S(1)}, f32[16,4096]{1,0:T(8,128)S(1)}, u32[]{:S(2)}, u32[]{:S(2)}) %collective-permute-start) | collective-permute-done | bytes 262176 | tf_op jit(solution)/shard_map/while/body/eval_jaxpr/ppermute | solution.py:9
  371.0 1.9 collective-permute-start
  373.0 9.6 %collective-permute-done = f32[16,4096]{1,0:T(8,128)S(1)} collective-permute-done((f32[16,4096]{1,0:T(8,128)S(1)}, f32[16,4096]{1,0:T(8,128)S(1)}, u32[]{:S(2)}, u32[]{:S(2)}) %collective-permute-start) | collective-permute-done | bytes 262176 | tf_op jit(solution)/shard_map/while/body/eval_jaxpr/ppermute | solution.py:9
  383.1 1.9 collective-permute-start
  385.1 9.6 %collective-permute-done = f32[16,4096]{1,0:T(8,128)S(1)} collective-permute-done((f32[16,4096]{1,0:T(8,128)S(1)}, f32[16,4096]{1,0:T(8,128)S(1)}, u32[]{:S(2)}, u32[]{:S(2)}) %collective-permute-start) | collective-permute-done | bytes 262176 | tf_op jit(solution)/shard_map/while/body/eval_jaxpr/ppermute | solution.py:9
  397.1 9.6 %collective-permute-done = f32[16,4096]{1,0:T(8,128)S(1)} collective-permute-done((f32[16,4096]{1,0:T(8,128)S(1)}, f32[16,4096]{1,0:T(8,128)S(1)}, u32[]{:S(2)}, u32[]{:S(2)}) %collective-permute-start) | collective-permute-done | bytes 262176 | tf_op jit(solution)/shard_map/while/body/eval_jaxpr/ppermute | solution.py:9
  407.3 1.9 collective-permute-start
  409.2 9.6 %collective-permute-done = f32[16,4096]{1,0:T(8,128)S(1)} collective-permute-done((f32[16,4096]{1,0:T(8,128)S(1)}, f32[16,4096]{1,0:T(8,128)S(1)}, u32[]{:S(2)}, u32[]{:S(2)}) %collective-permute-start) | collective-permute-done | bytes 262176 | tf_op jit(solution)/shard_map/while/body/eval_jaxpr/ppermute | solution.py:9
  419.3 1.9 collective-permute-start
  421.3 9.6 %collective-permute-done = f32[16,4096]{1,0:T(8,128)S(1)} collective-permute-done((f32[16,4096]{1,0:T(8,128)S(1)}, f32[16,4096]{1,0:T(8,128)S(1)}, u32[]{:S(2)}, u32[]{:S(2)}) %collective-permute-start) | collective-permute-done | bytes 262176 | tf_op jit(solution)/shard_map/while/body/eval_jaxpr/ppermute | solution.py:9
  431.4 1.9 collective-permute-start
  433.4 9.6 %collective-permute-done = f32[16,4096]{1,0:T(8,128)S(1)} collective-permute-done((f32[16,4096]{1,0:T(8,128)S(1)}, f32[16,4096]{1,0:T(8,128)S(1)}, u32[]{:S(2)}, u32[]{:S(2)}) %collective-permute-start) | collective-permute-done | bytes 262176 | tf_op jit(solution)/shard_map/while/body/eval_jaxpr/ppermute | solution.py:9
  443.5 1.9 collective-permute-start
  445.4 9.6 %collective-permute-done = f32[16,4096]{1,0:T(8,128)S(1)} collective-permute-done((f32[16,4096]{1,0:T(8,128)S(1)}, f32[16,4096]{1,0:T(8,128)S(1)}, u32[]{:S(2)}, u32[]{:S(2)}) %collective-permute-start) | collective-permute-done | bytes 262176 | tf_op jit(solution)/shard_map/while/body/eval_jaxpr/ppermute | solution.py:9
  455.6 1.9 collective-permute-start
  457.5 9.6 %collective-permute-done = f32[16,4096]{1,0:T(8,128)S(1)} collective-permute-done((f32[16,4096]{1,0:T(8,128)S(1)}, f32[16,4096]{1,0:T(8,128)S(1)}, u32[]{:S(2)}, u32[]{:S(2)}) %collective-permute-start) | collective-permute-done | bytes 262176 | tf_op jit(solution)/shard_map/while/body/eval_jaxpr/ppermute | solution.py:9
  469.6 9.6 %collective-permute-done = f32[16,4096]{1,0:T(8,128)S(1)} collective-permute-done((f32[16,4096]{1,0:T(8,128)S(1)}, f32[16,4096]{1,0:T(8,128)S(1)}, u32[]{:S(2)}, u32[]{:S(2)}) %collective-permute-start) | collective-permute-done | bytes 262176 | tf_op jit(solution)/shard_map/while/body/eval_jaxpr/ppermute | solution.py:9
  479.7 1.9 collective-permute-start
  481.7 9.6 %collective-permute-done = f32[16,4096]{1,0:T(8,128)S(1)} collective-permute-done((f32[16,4096]{1,0:T(8,128)S(1)}, f32[16,4096]{1,0:T(8,128)S(1)}, u32[]{:S(2)}, u32[]{:S(2)}) %collective-permute-start) | collective-permute-done | bytes 262176 | tf_op jit(solution)/shard_map/while/body/eval_jaxpr/ppermute | solution.py:9
  493.7 9.6 %collective-permute-done = f32[16,4096]{1,0:T(8,128)S(1)} collective-permute-done((f32[16,4096]{1,0:T(8,128)S(1)}, f32[16,4096]{1,0:T(8,128)S(1)}, u32[]{:S(2)}, u32[]{:S(2)}) %collective-permute-start) | collective-permute-done | bytes 262176 | tf_op jit(solution)/shard_map/while/body/eval_jaxpr/ppermute | solution.py:9
  503.9 1.9 collective-permute-start
  505.8 9.6 %collective-permute-done = f32[16,4096]{1,0:T(8,128)S(1)} collective-permute-done((f32[16,4096]{1,0:T(8,128)S(1)}, f32[16,4096]{1,0:T(8,128)S(1)}, u32[]{:S(2)}, u32[]{:S(2)}) %collective-permute-start) | collective-permute-done | bytes 262176 | tf_op jit(solution)/shard_map/while/body/eval_jaxpr/ppermute | solution.py:9
  517.9 9.6 %collective-permute-done = f32[16,4096]{1,0:T(8,128)S(1)} collective-permute-done((f32[16,4096]{1,0:T(8,128)S(1)}, f32[16,4096]{1,0:T(8,128)S(1)}, u32[]{:S(2)}, u32[]{:S(2)}) %collective-permute-start) | collective-permute-done | bytes 262176 | tf_op jit(solution)/shard_map/while/body/eval_jaxpr/ppermute | solution.py:9
  528.0 1.9 collective-permute-start
  530.0 9.6 %collective-permute-done = f32[16,4096]{1,0:T(8,128)S(1)} collective-permute-done((f32[16,4096]{1,0:T(8,128)S(1)}, f32[16,4096]{1,0:T(8,128)S(1)}, u32[]{:S(2)}, u32[]{:S(2)}) %collective-permute-start) | collective-permute-done | bytes 262176 | tf_op jit(solution)/shard_map/while/body/eval_jaxpr/ppermute | solution.py:9
  542.0 9.6 %collective-permute-done = f32[16,4096]{1,0:T(8,128)S(1)} collective-permute-done((f32[16,4096]{1,0:T(8,128)S(1)}, f32[16,4096]{1,0:T(8,128)S(1)}, u32[]{:S(2)}, u32[]{:S(2)}) %collective-permute-start) | collective-permute-done | bytes 262176 | tf_op jit(solution)/shard_map/while/body/eval_jaxpr/ppermute | solution.py:9
  554.1 9.6 %collective-permute-done = f32[16,4096]{1,0:T(8,128)S(1)} collective-permute-done((f32[16,4096]{1,0:T(8,128)S(1)}, f32[16,4096]{1,0:T(8,128)S(1)}, u32[]{:S(2)}, u32[]{:S(2)}) %collective-permute-start) | collective-permute-done | bytes 262176 | tf_op jit(solution)/shard_map/while/body/eval_jaxpr/ppermute | solution.py:9
  (70 shorter events, 41.3 us)
Async XLA Ops:
  0.6 21.3 %copy-start = (bf16[1,16,4096]{2,1,0:T(8,128)(2,1)S(1)}, bf16[1,16,4096]{2,1,0:T(8,128)(2,1)}, u32[]{:S(2)}) copy-start(bf16[1,16,4096]{2,1,0:T(8,128)(2,1)} %param.10) | copy-start | bytes 393220
  3.7 31.5 %all-to-all-start.1 = ((bf16[16,1,2]{2,1,0:T(2,128)(2,1)}), bf16[16,1,2]{2,1,0:T(2,128)(2,1)S(1)}, u32[]{:S(2)}, u32[]{:S(2)}) async-start(bf16[16,1,2]{2,1,0:T(2,128)(2,1)} %all_to_all.20), calls=%async_computation.1 | async-start | bytes 16384 | tf_op jit(solution)/shard_map/all_to_all | solution.py:41
  59.9 8.9 %copy-start.1 = (bf16[1,256,4096]{2,1,0:T(8,128)(2,1)S(1)}, bf16[1,256,4096]{2,1,0:T(8,128)(2,1)}, u32[]{:S(2)}) copy-start(bf16[1,256,4096]{2,1,0:T(8,128)(2,1)} %param.7) | copy-start | bytes 6291460
  59.9 102.5 %all-to-all-start = ((bf16[32,16,4096]{2,1,0:T(8,128)(2,1)}), bf16[32,16,4096]{2,1,0:T(8,128)(2,1)}, u32[]{:S(2)}, u32[]{:S(2)}) async-start(bf16[32,16,4096]{2,1,0:T(8,128)(2,1)} %stack.3), calls=%async_computation | async-start | bytes 8388608 | tf_op jit(solution)/shard_map/all_to_all | solution.py:57
  162.5 3.6 copy-start.2
  177.4 387.5 %all-to-all-start.3 = ((bf16[16,2,4096]{2,1,0:T(2,128)(2,1)}), bf16[16,2,4096]{2,1,0:T(2,128)(2,1)S(1)}, u32[]{:S(2)}, u32[]{:S(2)}) async-start(bf16[16,2,4096]{2,1,0:T(2,128)(2,1)} %reshape.106), calls=%async_computation.3 | async-start | bytes 524288 | tf_op jit(solution)/shard_map/all_to_all | solution.py:103
  184.3 17.2 %collective-permute-start = (f32[16,4096]{1,0:T(8,128)S(1)}, f32[16,4096]{1,0:T(8,128)S(1)}, u32[]{:S(2)}, u32[]{:S(2)}) collective-permute-start(f32[16,4096]{1,0:T(8,128)S(1)} %get-tuple-element.201), channel_id=1, source_target_pairs={{0,16},{16,32},{32,48},{48,64},{64,80},{80,96},{96,112},{112,128},... | collective-permute-start | bytes 786440 | tf_op jit(solution)/shard_map/while/body/eval_jaxpr/ppermute | solution.py:9
  202.0 11.6 %collective-permute-start = (f32[16,4096]{1,0:T(8,128)S(1)}, f32[16,4096]{1,0:T(8,128)S(1)}, u32[]{:S(2)}, u32[]{:S(2)}) collective-permute-start(f32[16,4096]{1,0:T(8,128)S(1)} %get-tuple-element.201), channel_id=1, source_target_pairs={{0,16},{16,32},{32,48},{48,64},{64,80},{80,96},{96,112},{112,128},... | collective-permute-start | bytes 786440 | tf_op jit(solution)/shard_map/while/body/eval_jaxpr/ppermute | solution.py:9
  214.1 11.6 %collective-permute-start = (f32[16,4096]{1,0:T(8,128)S(1)}, f32[16,4096]{1,0:T(8,128)S(1)}, u32[]{:S(2)}, u32[]{:S(2)}) collective-permute-start(f32[16,4096]{1,0:T(8,128)S(1)} %get-tuple-element.201), channel_id=1, source_target_pairs={{0,16},{16,32},{32,48},{48,64},{64,80},{80,96},{96,112},{112,128},... | collective-permute-start | bytes 786440 | tf_op jit(solution)/shard_map/while/body/eval_jaxpr/ppermute | solution.py:9
  226.1 11.6 %collective-permute-start = (f32[16,4096]{1,0:T(8,128)S(1)}, f32[16,4096]{1,0:T(8,128)S(1)}, u32[]{:S(2)}, u32[]{:S(2)}) collective-permute-start(f32[16,4096]{1,0:T(8,128)S(1)} %get-tuple-element.201), channel_id=1, source_target_pairs={{0,16},{16,32},{32,48},{48,64},{64,80},{80,96},{96,112},{112,128},... | collective-permute-start | bytes 786440 | tf_op jit(solution)/shard_map/while/body/eval_jaxpr/ppermute | solution.py:9
  238.2 11.6 %collective-permute-start = (f32[16,4096]{1,0:T(8,128)S(1)}, f32[16,4096]{1,0:T(8,128)S(1)}, u32[]{:S(2)}, u32[]{:S(2)}) collective-permute-start(f32[16,4096]{1,0:T(8,128)S(1)} %get-tuple-element.201), channel_id=1, source_target_pairs={{0,16},{16,32},{32,48},{48,64},{64,80},{80,96},{96,112},{112,128},... | collective-permute-start | bytes 786440 | tf_op jit(solution)/shard_map/while/body/eval_jaxpr/ppermute | solution.py:9
  250.3 11.6 %collective-permute-start = (f32[16,4096]{1,0:T(8,128)S(1)}, f32[16,4096]{1,0:T(8,128)S(1)}, u32[]{:S(2)}, u32[]{:S(2)}) collective-permute-start(f32[16,4096]{1,0:T(8,128)S(1)} %get-tuple-element.201), channel_id=1, source_target_pairs={{0,16},{16,32},{32,48},{48,64},{64,80},{80,96},{96,112},{112,128},... | collective-permute-start | bytes 786440 | tf_op jit(solution)/shard_map/while/body/eval_jaxpr/ppermute | solution.py:9
  262.4 11.6 %collective-permute-start = (f32[16,4096]{1,0:T(8,128)S(1)}, f32[16,4096]{1,0:T(8,128)S(1)}, u32[]{:S(2)}, u32[]{:S(2)}) collective-permute-start(f32[16,4096]{1,0:T(8,128)S(1)} %get-tuple-element.201), channel_id=1, source_target_pairs={{0,16},{16,32},{32,48},{48,64},{64,80},{80,96},{96,112},{112,128},... | collective-permute-start | bytes 786440 | tf_op jit(solution)/shard_map/while/body/eval_jaxpr/ppermute | solution.py:9
  274.4 11.6 %collective-permute-start = (f32[16,4096]{1,0:T(8,128)S(1)}, f32[16,4096]{1,0:T(8,128)S(1)}, u32[]{:S(2)}, u32[]{:S(2)}) collective-permute-start(f32[16,4096]{1,0:T(8,128)S(1)} %get-tuple-element.201), channel_id=1, source_target_pairs={{0,16},{16,32},{32,48},{48,64},{64,80},{80,96},{96,112},{112,128},... | collective-permute-start | bytes 786440 | tf_op jit(solution)/shard_map/while/body/eval_jaxpr/ppermute | solution.py:9
  286.5 11.6 %collective-permute-start = (f32[16,4096]{1,0:T(8,128)S(1)}, f32[16,4096]{1,0:T(8,128)S(1)}, u32[]{:S(2)}, u32[]{:S(2)}) collective-permute-start(f32[16,4096]{1,0:T(8,128)S(1)} %get-tuple-element.201), channel_id=1, source_target_pairs={{0,16},{16,32},{32,48},{48,64},{64,80},{80,96},{96,112},{112,128},... | collective-permute-start | bytes 786440 | tf_op jit(solution)/shard_map/while/body/eval_jaxpr/ppermute | solution.py:9
  298.6 11.6 %collective-permute-start = (f32[16,4096]{1,0:T(8,128)S(1)}, f32[16,4096]{1,0:T(8,128)S(1)}, u32[]{:S(2)}, u32[]{:S(2)}) collective-permute-start(f32[16,4096]{1,0:T(8,128)S(1)} %get-tuple-element.201), channel_id=1, source_target_pairs={{0,16},{16,32},{32,48},{48,64},{64,80},{80,96},{96,112},{112,128},... | collective-permute-start | bytes 786440 | tf_op jit(solution)/shard_map/while/body/eval_jaxpr/ppermute | solution.py:9
  310.7 11.6 %collective-permute-start = (f32[16,4096]{1,0:T(8,128)S(1)}, f32[16,4096]{1,0:T(8,128)S(1)}, u32[]{:S(2)}, u32[]{:S(2)}) collective-permute-start(f32[16,4096]{1,0:T(8,128)S(1)} %get-tuple-element.201), channel_id=1, source_target_pairs={{0,16},{16,32},{32,48},{48,64},{64,80},{80,96},{96,112},{112,128},... | collective-permute-start | bytes 786440 | tf_op jit(solution)/shard_map/while/body/eval_jaxpr/ppermute | solution.py:9
  322.7 11.6 %collective-permute-start = (f32[16,4096]{1,0:T(8,128)S(1)}, f32[16,4096]{1,0:T(8,128)S(1)}, u32[]{:S(2)}, u32[]{:S(2)}) collective-permute-start(f32[16,4096]{1,0:T(8,128)S(1)} %get-tuple-element.201), channel_id=1, source_target_pairs={{0,16},{16,32},{32,48},{48,64},{64,80},{80,96},{96,112},{112,128},... | collective-permute-start | bytes 786440 | tf_op jit(solution)/shard_map/while/body/eval_jaxpr/ppermute | solution.py:9
  334.8 11.6 %collective-permute-start = (f32[16,4096]{1,0:T(8,128)S(1)}, f32[16,4096]{1,0:T(8,128)S(1)}, u32[]{:S(2)}, u32[]{:S(2)}) collective-permute-start(f32[16,4096]{1,0:T(8,128)S(1)} %get-tuple-element.201), channel_id=1, source_target_pairs={{0,16},{16,32},{32,48},{48,64},{64,80},{80,96},{96,112},{112,128},... | collective-permute-start | bytes 786440 | tf_op jit(solution)/shard_map/while/body/eval_jaxpr/ppermute | solution.py:9
  346.9 11.6 %collective-permute-start = (f32[16,4096]{1,0:T(8,128)S(1)}, f32[16,4096]{1,0:T(8,128)S(1)}, u32[]{:S(2)}, u32[]{:S(2)}) collective-permute-start(f32[16,4096]{1,0:T(8,128)S(1)} %get-tuple-element.201), channel_id=1, source_target_pairs={{0,16},{16,32},{32,48},{48,64},{64,80},{80,96},{96,112},{112,128},... | collective-permute-start | bytes 786440 | tf_op jit(solution)/shard_map/while/body/eval_jaxpr/ppermute | solution.py:9
  359.0 11.6 %collective-permute-start = (f32[16,4096]{1,0:T(8,128)S(1)}, f32[16,4096]{1,0:T(8,128)S(1)}, u32[]{:S(2)}, u32[]{:S(2)}) collective-permute-start(f32[16,4096]{1,0:T(8,128)S(1)} %get-tuple-element.201), channel_id=1, source_target_pairs={{0,16},{16,32},{32,48},{48,64},{64,80},{80,96},{96,112},{112,128},... | collective-permute-start | bytes 786440 | tf_op jit(solution)/shard_map/while/body/eval_jaxpr/ppermute | solution.py:9
  371.0 11.6 %collective-permute-start = (f32[16,4096]{1,0:T(8,128)S(1)}, f32[16,4096]{1,0:T(8,128)S(1)}, u32[]{:S(2)}, u32[]{:S(2)}) collective-permute-start(f32[16,4096]{1,0:T(8,128)S(1)} %get-tuple-element.201), channel_id=1, source_target_pairs={{0,16},{16,32},{32,48},{48,64},{64,80},{80,96},{96,112},{112,128},... | collective-permute-start | bytes 786440 | tf_op jit(solution)/shard_map/while/body/eval_jaxpr/ppermute | solution.py:9
  383.1 11.6 %collective-permute-start = (f32[16,4096]{1,0:T(8,128)S(1)}, f32[16,4096]{1,0:T(8,128)S(1)}, u32[]{:S(2)}, u32[]{:S(2)}) collective-permute-start(f32[16,4096]{1,0:T(8,128)S(1)} %get-tuple-element.201), channel_id=1, source_target_pairs={{0,16},{16,32},{32,48},{48,64},{64,80},{80,96},{96,112},{112,128},... | collective-permute-start | bytes 786440 | tf_op jit(solution)/shard_map/while/body/eval_jaxpr/ppermute | solution.py:9
  395.2 11.6 %collective-permute-start = (f32[16,4096]{1,0:T(8,128)S(1)}, f32[16,4096]{1,0:T(8,128)S(1)}, u32[]{:S(2)}, u32[]{:S(2)}) collective-permute-start(f32[16,4096]{1,0:T(8,128)S(1)} %get-tuple-element.201), channel_id=1, source_target_pairs={{0,16},{16,32},{32,48},{48,64},{64,80},{80,96},{96,112},{112,128},... | collective-permute-start | bytes 786440 | tf_op jit(solution)/shard_map/while/body/eval_jaxpr/ppermute | solution.py:9
  407.3 11.6 %collective-permute-start = (f32[16,4096]{1,0:T(8,128)S(1)}, f32[16,4096]{1,0:T(8,128)S(1)}, u32[]{:S(2)}, u32[]{:S(2)}) collective-permute-start(f32[16,4096]{1,0:T(8,128)S(1)} %get-tuple-element.201), channel_id=1, source_target_pairs={{0,16},{16,32},{32,48},{48,64},{64,80},{80,96},{96,112},{112,128},... | collective-permute-start | bytes 786440 | tf_op jit(solution)/shard_map/while/body/eval_jaxpr/ppermute | solution.py:9
  419.3 11.6 %collective-permute-start = (f32[16,4096]{1,0:T(8,128)S(1)}, f32[16,4096]{1,0:T(8,128)S(1)}, u32[]{:S(2)}, u32[]{:S(2)}) collective-permute-start(f32[16,4096]{1,0:T(8,128)S(1)} %get-tuple-element.201), channel_id=1, source_target_pairs={{0,16},{16,32},{32,48},{48,64},{64,80},{80,96},{96,112},{112,128},... | collective-permute-start | bytes 786440 | tf_op jit(solution)/shard_map/while/body/eval_jaxpr/ppermute | solution.py:9
  431.4 11.6 %collective-permute-start = (f32[16,4096]{1,0:T(8,128)S(1)}, f32[16,4096]{1,0:T(8,128)S(1)}, u32[]{:S(2)}, u32[]{:S(2)}) collective-permute-start(f32[16,4096]{1,0:T(8,128)S(1)} %get-tuple-element.201), channel_id=1, source_target_pairs={{0,16},{16,32},{32,48},{48,64},{64,80},{80,96},{96,112},{112,128},... | collective-permute-start | bytes 786440 | tf_op jit(solution)/shard_map/while/body/eval_jaxpr/ppermute | solution.py:9
  443.5 11.6 %collective-permute-start = (f32[16,4096]{1,0:T(8,128)S(1)}, f32[16,4096]{1,0:T(8,128)S(1)}, u32[]{:S(2)}, u32[]{:S(2)}) collective-permute-start(f32[16,4096]{1,0:T(8,128)S(1)} %get-tuple-element.201), channel_id=1, source_target_pairs={{0,16},{16,32},{32,48},{48,64},{64,80},{80,96},{96,112},{112,128},... | collective-permute-start | bytes 786440 | tf_op jit(solution)/shard_map/while/body/eval_jaxpr/ppermute | solution.py:9
  455.6 11.6 %collective-permute-start = (f32[16,4096]{1,0:T(8,128)S(1)}, f32[16,4096]{1,0:T(8,128)S(1)}, u32[]{:S(2)}, u32[]{:S(2)}) collective-permute-start(f32[16,4096]{1,0:T(8,128)S(1)} %get-tuple-element.201), channel_id=1, source_target_pairs={{0,16},{16,32},{32,48},{48,64},{64,80},{80,96},{96,112},{112,128},... | collective-permute-start | bytes 786440 | tf_op jit(solution)/shard_map/while/body/eval_jaxpr/ppermute | solution.py:9
  467.6 11.6 %collective-permute-start = (f32[16,4096]{1,0:T(8,128)S(1)}, f32[16,4096]{1,0:T(8,128)S(1)}, u32[]{:S(2)}, u32[]{:S(2)}) collective-permute-start(f32[16,4096]{1,0:T(8,128)S(1)} %get-tuple-element.201), channel_id=1, source_target_pairs={{0,16},{16,32},{32,48},{48,64},{64,80},{80,96},{96,112},{112,128},... | collective-permute-start | bytes 786440 | tf_op jit(solution)/shard_map/while/body/eval_jaxpr/ppermute | solution.py:9
  479.7 11.6 %collective-permute-start = (f32[16,4096]{1,0:T(8,128)S(1)}, f32[16,4096]{1,0:T(8,128)S(1)}, u32[]{:S(2)}, u32[]{:S(2)}) collective-permute-start(f32[16,4096]{1,0:T(8,128)S(1)} %get-tuple-element.201), channel_id=1, source_target_pairs={{0,16},{16,32},{32,48},{48,64},{64,80},{80,96},{96,112},{112,128},... | collective-permute-start | bytes 786440 | tf_op jit(solution)/shard_map/while/body/eval_jaxpr/ppermute | solution.py:9
  491.8 11.6 %collective-permute-start = (f32[16,4096]{1,0:T(8,128)S(1)}, f32[16,4096]{1,0:T(8,128)S(1)}, u32[]{:S(2)}, u32[]{:S(2)}) collective-permute-start(f32[16,4096]{1,0:T(8,128)S(1)} %get-tuple-element.201), channel_id=1, source_target_pairs={{0,16},{16,32},{32,48},{48,64},{64,80},{80,96},{96,112},{112,128},... | collective-permute-start | bytes 786440 | tf_op jit(solution)/shard_map/while/body/eval_jaxpr/ppermute | solution.py:9
  503.9 11.6 %collective-permute-start = (f32[16,4096]{1,0:T(8,128)S(1)}, f32[16,4096]{1,0:T(8,128)S(1)}, u32[]{:S(2)}, u32[]{:S(2)}) collective-permute-start(f32[16,4096]{1,0:T(8,128)S(1)} %get-tuple-element.201), channel_id=1, source_target_pairs={{0,16},{16,32},{32,48},{48,64},{64,80},{80,96},{96,112},{112,128},... | collective-permute-start | bytes 786440 | tf_op jit(solution)/shard_map/while/body/eval_jaxpr/ppermute | solution.py:9
  515.9 11.6 %collective-permute-start = (f32[16,4096]{1,0:T(8,128)S(1)}, f32[16,4096]{1,0:T(8,128)S(1)}, u32[]{:S(2)}, u32[]{:S(2)}) collective-permute-start(f32[16,4096]{1,0:T(8,128)S(1)} %get-tuple-element.201), channel_id=1, source_target_pairs={{0,16},{16,32},{32,48},{48,64},{64,80},{80,96},{96,112},{112,128},... | collective-permute-start | bytes 786440 | tf_op jit(solution)/shard_map/while/body/eval_jaxpr/ppermute | solution.py:9
  528.0 11.6 %collective-permute-start = (f32[16,4096]{1,0:T(8,128)S(1)}, f32[16,4096]{1,0:T(8,128)S(1)}, u32[]{:S(2)}, u32[]{:S(2)}) collective-permute-start(f32[16,4096]{1,0:T(8,128)S(1)} %get-tuple-element.201), channel_id=1, source_target_pairs={{0,16},{16,32},{32,48},{48,64},{64,80},{80,96},{96,112},{112,128},... | collective-permute-start | bytes 786440 | tf_op jit(solution)/shard_map/while/body/eval_jaxpr/ppermute | solution.py:9
  540.1 11.6 %collective-permute-start = (f32[16,4096]{1,0:T(8,128)S(1)}, f32[16,4096]{1,0:T(8,128)S(1)}, u32[]{:S(2)}, u32[]{:S(2)}) collective-permute-start(f32[16,4096]{1,0:T(8,128)S(1)} %get-tuple-element.201), channel_id=1, source_target_pairs={{0,16},{16,32},{32,48},{48,64},{64,80},{80,96},{96,112},{112,128},... | collective-permute-start | bytes 786440 | tf_op jit(solution)/shard_map/while/body/eval_jaxpr/ppermute | solution.py:9
  552.2 11.6 %collective-permute-start = (f32[16,4096]{1,0:T(8,128)S(1)}, f32[16,4096]{1,0:T(8,128)S(1)}, u32[]{:S(2)}, u32[]{:S(2)}) collective-permute-start(f32[16,4096]{1,0:T(8,128)S(1)} %get-tuple-element.201), channel_id=1, source_target_pairs={{0,16},{16,32},{32,48},{48,64},{64,80},{80,96},{96,112},{112,128},... | collective-permute-start | bytes 786440 | tf_op jit(solution)/shard_map/while/body/eval_jaxpr/ppermute | solution.py:9
